TPU v7x, 256 devices: a whole 4x4x8 slice. The times are simulated.
256 devices in a mesh: req: 32 (over y, x, z_hi), tp: 8 (over z_lo, core).
Axes of the slice: x: 4, y: 4, z: 8 (z_hi: 2, z_lo: 4; z = z_hi * 4 + z_lo), core: 2. Of those that a mesh axis runs over, the one named last changes fastest.
Arguments:
- residual: bfloat16 [8192, 2304], P('req'), may hold values from -58 to 58
- context: bfloat16 [8192, 2304], P('req', 'tp'), may hold values from -6 to 6
- attention_output_weight: bfloat16 [2304, 2304], P('tp'), may hold values from -0.1875 to 0.1875
- adapter_down_maps: bfloat16 [64, 2304, 16], P('req', 'tp'), may hold values from -0.125 to 0.125
- adapter_up_maps: bfloat16 [64, 16, 2304], P('req'), may hold values from -1.5 to 1.5
- adapter_storage_row: int32 [64], replicated, may hold values from 0 to 63, each once
- active_adapters: int32 [16], replicated, may hold values from 0 to 63, as said below
- request_token_length: int32 [32, 4], P('req'), may hold values from 1 to 128, 256 in all within a row
- request_adapter_entry: int32 [32, 4], P('req'), may hold values from 0 to 15
- expert_norm_gain: bfloat16 [2304], replicated, may hold values from 0.099609375 to 1.8984375
- router_projection: bfloat16 [2304, 8], replicated, may hold values from -0.125 to 0.125
- expert_choice_pairs: int32 [8192, 2], P('req'), may hold values from 0 to 7, all different within a row; in each aligned block of 256 rows (0 to 255, 256 to 511, ...) at most 80 rows name the same one
- expert_gate_weight: bfloat16 [32, 2304, 5760], P('req', None, 'tp'), as said below
- expert_up_weight: bfloat16 [32, 2304, 5760], P('req', None, 'tp'), as said below
- expert_down_weight: bfloat16 [32, 5760, 2304], P('req', 'tp'), as said below
Outputs:
- layer_out: bfloat16 [8192, 2304], P('req', 'tp')
Inputs may be any that keep to these rules, and one draw needn't show every extreme that they name: `active_adapters`: 16 different adapter numbers, 0 and 63 among them. `adapter_storage_row`: every stored row appears once. `request_token_length`: each group's lengths sum to 256; the longest request of a group has exactly half of 256 tokens. `expert_choice_pairs`: each row names two different experts; within the 256 rows of one group no expert is named by more than 80 rows, a bound that some block reaches. `expert_gate_weight`: the 4 holders c * 8 + e of expert e hold the same weights. `expert_up_weight`: the 4 holders c * 8 + e of expert e hold the same weights. `expert_down_weight`: the 4 holders c * 8 + e of expert e hold the same weights.
All inputs are finite; a program needn't handle non-finite values.
Results may differ from a plain program's by a relative error of at most 0.0095.
Values may be sent and summed in bfloat16 or wider, within the bound.
A program may use at most 128 MiB of HBM per device.

v0:
```python
import jax
import jax.numpy as jnp
from jax import lax
from jax.sharding import PartitionSpec as P

CAP = 80
NORM_EPS = 1e-05


def adapter_onehot(request_token_length, request_adapter_entry, active_count, token_count):
    bounds = jnp.cumsum(request_token_length[0])
    position = jnp.arange(token_count, dtype=jnp.int32)
    segment = jnp.sum((position[:, None] >= bounds[None, :]).astype(jnp.int32), axis=1)
    slot_range = jnp.arange(request_token_length.shape[1], dtype=jnp.int32)
    segment_hot = (segment[:, None] == slot_range[None, :]).astype(jnp.int32)
    token_pick = jnp.sum(segment_hot * request_adapter_entry[0][None, :], axis=1)
    return token_pick[:, None] == jnp.arange(active_count, dtype=jnp.int32)[None, :]


def route_tables(expert_choice_pairs, expert_count, capacity):
    expert_ids = jnp.arange(expert_count, dtype=jnp.int32)
    first_hit = expert_choice_pairs[None, :, 0] == expert_ids[:, None]
    second_hit = expert_choice_pairs[None, :, 1] == expert_ids[:, None]
    chosen = first_hit | second_hit
    slot_of = jnp.cumsum(chosen.astype(jnp.int32), axis=1) - 1
    slot_range = jnp.arange(capacity, dtype=jnp.int32)
    placement = chosen[:, None, :] & (slot_of[:, None, :] == slot_range[None, :, None])
    return (placement, first_hit, second_hit)


def on_device(
    residual,
    context,
    attention_output_weight,
    adapter_down_maps,
    adapter_up_maps,
    adapter_storage_row,
    active_adapters,
    request_token_length,
    request_adapter_entry,
    expert_norm_gain,
    router_projection,
    expert_choice_pairs,
    expert_gate_weight,
    expert_up_weight,
    expert_down_weight,
):
    token_count = residual.shape[0]
    hidden_width = residual.shape[1]
    active_count = active_adapters.shape[0]
    adapter_rank_size = adapter_down_maps.shape[2]
    stored_rows = adapter_storage_row[active_adapters]
    all_down, all_up = (
        lax.all_gather(adapter_down_maps, "req", axis=0, tiled=True),
        lax.all_gather(adapter_up_maps, "req", axis=0, tiled=True),
    )
    active_down = all_down[stored_rows]
    active_up = all_up[stored_rows]
    adapter_indicator = adapter_onehot(
        request_token_length, request_adapter_entry, active_count, token_count
    )
    down_joined = jnp.transpose(active_down, (1, 0, 2)).reshape(
        context.shape[1], active_count * adapter_rank_size
    )
    up_joined = active_up.reshape(active_count * adapter_rank_size, hidden_width)
    low_all = jnp.dot(context, down_joined, preferred_element_type=jnp.float32)
    reduced_mask = jnp.repeat(adapter_indicator, adapter_rank_size, axis=1)
    low_rank = jnp.where(reduced_mask, low_all, 0.0).astype(jnp.bfloat16)
    head_part = jnp.dot(
        context, attention_output_weight, preferred_element_type=jnp.float32
    ) + jnp.dot(low_rank, up_joined, preferred_element_type=jnp.float32)
    share_width = hidden_width // lax.axis_size("tp")
    share_start = lax.axis_index("tp") * share_width
    gain_all = expert_norm_gain.astype(jnp.float32)
    head_sum = lax.psum(head_part.astype(jnp.bfloat16), "tp").astype(jnp.float32)
    blended_rows = residual.astype(jnp.float32) + head_sum
    mean_square = jnp.mean(blended_rows * blended_rows, axis=1, keepdims=True)
    normed = (blended_rows * lax.rsqrt(mean_square + NORM_EPS) * gain_all).astype(jnp.bfloat16)
    mixed_share = lax.dynamic_slice_in_dim(blended_rows, share_start, share_width, 1)
    logits = jnp.dot(normed, router_projection, preferred_element_type=jnp.float32)
    expert_count = router_projection.shape[1]
    expert_range = jnp.arange(expert_count, dtype=jnp.int32)
    logit_first = jnp.sum(
        jnp.where(expert_choice_pairs[:, 0:1] == expert_range[None, :], logits, 0.0), axis=1
    )
    logit_second = jnp.sum(
        jnp.where(expert_choice_pairs[:, 1:2] == expert_range[None, :], logits, 0.0), axis=1
    )
    weight_first = 1.0 / (1.0 + jnp.exp(logit_second - logit_first))
    weight_second = 1.0 / (1.0 + jnp.exp(logit_first - logit_second))
    copy_count = lax.axis_size("req") // expert_count
    quota_slots = CAP // copy_count
    placement, first_hit, second_hit = route_tables(expert_choice_pairs, expert_count, CAP)
    holder_place = jnp.transpose(
        placement.reshape(expert_count, copy_count, quota_slots, token_count), (1, 0, 2, 3)
    ).reshape(copy_count * expert_count, quota_slots, token_count)
    send_rows = jnp.einsum(
        "hqt,td->hqd", holder_place.astype(jnp.bfloat16), normed, preferred_element_type=jnp.float32
    ).astype(jnp.bfloat16)
    gate_local = expert_gate_weight[0]
    up_local = expert_up_weight[0]
    down_local = expert_down_weight[0]
    rows_in = lax.all_to_all(send_rows, "req", split_axis=0, concat_axis=0, tiled=True)
    gate_value = jnp.einsum("nqd,df->nqf", rows_in, gate_local, preferred_element_type=jnp.float32)
    up_value = jnp.einsum("nqd,df->nqf", rows_in, up_local, preferred_element_type=jnp.float32)
    hidden = (jax.nn.silu(gate_value) * up_value).astype(jnp.bfloat16)
    partial_value = jnp.einsum(
        "nqf,fd->nqd", hidden, down_local, preferred_element_type=jnp.float32
    )
    token_weight = jnp.where(first_hit, weight_first[None, :], 0.0) + jnp.where(
        second_hit, weight_second[None, :], 0.0
    )
    holder_weight = jnp.tile(token_weight, (copy_count, 1))
    scaled_place = holder_place.astype(jnp.float32) * holder_weight[:, None, :]
    returned = lax.all_to_all(
        partial_value.astype(jnp.bfloat16), "req", split_axis=0, concat_axis=0, tiled=True
    )
    contribution = jnp.einsum(
        "hqt,hqd->td",
        scaled_place,
        returned.astype(jnp.float32),
        precision=lax.Precision.HIGHEST,
        preferred_element_type=jnp.float32,
    )
    moe_share = lax.psum_scatter(
        contribution.astype(jnp.bfloat16), "tp", scatter_dimension=1, tiled=True
    ).astype(jnp.float32)
    return (mixed_share + moe_share).astype(jnp.bfloat16)


def solution(mesh):
    return jax.shard_map(
        on_device,
        mesh=mesh,
        in_specs=(
            P("req", None),
            P("req", "tp"),
            P("tp", None),
            P("req", "tp", None),
            P("req", None, None),
            P(),
            P(),
            P("req", None),
            P("req", None),
            P(),
            P(),
            P("req", None),
            P("req", None, "tp"),
            P("req", None, "tp"),
            P("req", "tp", None),
        ),
        out_specs=P("req", "tp"),
        check_vma=False,
    )
```

profile of v0, /device:TPU:4, one launch (start us, length us, event | category | flops | bytes accessed | tf_op | source)
XLA Modules:
  0.0 505.3 jit_solution(13145580559629970987)
XLA Ops:
  6.5 0.0 copy-start
  6.5 0.0 all-gather.2.cloned.1.call-start
  6.5 0.7 all-gather.2.cloned.1.call-update
  7.3 0.0 all-reduce.2.cloned.1.call-start
  7.3 0.9 convert_element_type.53
  8.2 1.3 reduce-window.18
  9.6 0.8 fusion.41
  10.3 0.6 reduce-window.19
  10.9 0.2 slice_reduce_fusion
  11.2 0.0 copy-start.4
  11.2 0.7 compare_select_fusion.1
  11.8 1.3 gather_fusion
  13.2 136.1 %all_gather.6 = bf16[64,288,16]{1,2,0:T(8,128)(2,1)} all-gather(bf16[2,288,16]{1,2,0:T(8,128)(2,1)} %param.18), channel_id=1, replica_groups=mesh['req'=32,'tp'=8] {'req'}, dimensions={0}, use_global_device_ids=true | all-gather | bytes 608256 | tf_op jit(solution)/shard_map/all_gather | solution.py:54
  149.3 1.7 gather_fusion.1
  151.0 0.7 convert_reduce_fusion
  151.7 0.7 select_reduce_fusion.2
  152.5 3.7 fusion.42
  156.1 0.0 copy-done.4
  156.1 0.0 all-gather.2.cloned.1.call-done
  156.2 4.0 gather_fusion.2
  160.1 0.6 broadcast_in_dim.27
  160.8 0.0 slice-start
  160.8 3.9 fusion.1
  164.7 0.0 all-reduce.2.cloned.1.call-update
  164.8 0.1 copy.29
  164.9 0.0 slice-done
  164.9 0.1 add_bitcast_fusion
  165.0 77.7 %all-reduce.2.cloned.1.call-done = bf16[256,2304]{1,0:T(8,128)(2,1)} async-done(((bf16[256,2304]{1,0:T(8,128)(2,1)}), bf16[256,2304]{1,0:T(8,128)(2,1)}) %all-reduce.2.cloned.1.call-update) | async-done | bytes 1179664 | tf_op jit(solution)/shard_map/psum | solution.py:75
  242.6 0.0 copy-start.1
  242.6 0.0 copy-start.2
  242.6 3.6 convert_add_fusion
  246.2 0.0 copy-done.1
  246.2 0.0 copy-done.2
  246.2 1.2 convolution_convert_fusion.1
  247.4 1.6 copy.30
  249.0 0.0 copy-start.5
  249.0 91.9 %all_to_all.10 = bf16[32,20,2304]{2,1,0:T(8,128)(2,1)S(1)} all-to-all(bf16[32,20,2304]{2,1,0:T(8,128)(2,1)S(1)} %copy.30), channel_id=1, replica_groups=mesh['req'=32,'tp'=8] {'req'}, dimensions={0} | all-to-all | bytes 5898240 | tf_op jit(solution)/shard_map/all_to_all | solution.py:103
  340.9 0.0 copy-start.3
  340.9 1.8 copy-done.3
  342.7 0.0 copy-done.5
  342.7 3.8 fusion.6
  346.5 0.0 copy-done
  346.5 11.1 %convolution_convert_fusion = bf16[32,20,2304]{2,0,1:T(8,128)(2,1)} fusion(bf16[1,720,2304]{2,1,0:T(8,128)(2,1)S(1)} %copy-done, f32[32,20,720]{2,0,1:T(8,128)} %fusion.6, bf16[1,2304,720]{1,2,0:T(8,128)(2,1)} %param.28, bf16[32,20,2304]{2,1,0:T(8,128)(2,1)} %copy-done.3), kind=kOutput, calls=%fused_computation.3 | convolution fusion | flops 4250972160 | bytes 14376960 | tf_op jit(solution)/shard_map/nqf,fd->nqd/dot_general | solution.py:107
  357.6 5.3 %copy.33 = bf16[32,20,2304]{2,1,0:T(8,128)(2,1)} copy(bf16[32,20,2304]{2,0,1:T(8,128)(2,1)} %convolution_convert_fusion) | data formatting | bytes 5898240 | tf_op jit(solution)/shard_map/convert_element_type | solution.py:116
  362.9 0.0 copy-start.6
  362.9 8.3 %all-to-all-start.1 = ((bf16[32,20,2304]{2,1,0:T(8,128)(2,1)}), bf16[32,20,2304]{2,1,0:T(8,128)(2,1)}, u32[]{:S(2)}, u32[]{:S(2)}) async-start(bf16[32,20,2304]{2,1,0:T(8,128)(2,1)} %copy.33), calls=%async_computation.1 | async-start | bytes 7077888 | tf_op jit(solution)/shard_map/all_to_all | solution.py:115
  371.2 0.3 reduce-scatter.4.cloned.1.call-start
  371.5 0.0 copy-done.6
  371.5 2.2 select_reduce_fusion.1
  373.8 67.8 %all-to-all-done.1 = bf16[32,20,2304]{2,1,0:T(8,128)(2,1)} async-done(((bf16[32,20,2304]{2,1,0:T(8,128)(2,1)}), bf16[32,20,2304]{2,1,0:T(8,128)(2,1)}, u32[]{:S(2)}, u32[]{:S(2)}) %all-to-all-start.1) | async-done | bytes 2949152 | tf_op jit(solution)/shard_map/all_to_all | solution.py:115
  441.5 6.8 %fusion.2 = bf16[2304,256]{1,0:T(8,128)(2,1)} fusion(bf16[32,20,2304]{2,1,0:T(8,128)(2,1)} %all-to-all-done.1, f32[32,256]{1,0:T(8,128)S(1)} %broadcast_bitcast_fusion, s32[32,20]{0,1:T(8,128)S(1)} %copy.29, s32[32,256]{1,0:T(8,128)S(1)} %broadcast_bitcast_fusion.1, pred[32,256]{1,0:T(8,128)(4,1)S(1)} %broadcast_bitcast_fusion.2), kind=kOutput, calls=%fused_computation.9 | convolution fusion | flops 4530929664 | bytes 4205056 | tf_op jit(solution)/shard_map/hqt,hqd->td/dot_general | solution.py:118
  448.3 0.0 reduce-scatter.4.cloned.1.call-update
  448.3 45.8 %reduce-scatter.4.cloned.1.call-done = bf16[288,256]{1,0:T(8,128)(2,1)} async-done(((bf16[2304,256]{1,0:T(8,128)(2,1)}), bf16[288,256]{1,0:T(8,128)(2,1)}) %reduce-scatter.4.cloned.1.call-update) | async-done | bytes 147472
  494.1 1.1 copy.38
  495.2 1.9 add_convert_fusion
  497.1 1.7 copy.36
  (15 shorter events, 0.1 us)
Async XLA Ops:
  6.5 340.0 %copy-start = (bf16[1,720,2304]{2,1,0:T(8,128)(2,1)S(1)}, bf16[1,720,2304]{2,1,0:T(8,128)(2,1)}, u32[]{:S(2)}) copy-start(bf16[1,720,2304]{2,1,0:T(8,128)(2,1)} %param.29) | copy-start | bytes 9953284
  6.5 149.6 %all-gather.2.cloned.1.call-start = ((), (), s32[]{:S(2)}) async-start(), calls=%async_computation.3 | async-start | bytes 4866048 | tf_op jit(solution)/shard_map/all_gather | solution.py:55
  7.3 235.3 %all-reduce.2.cloned.1.call-start = ((), (), s32[]{:S(2)}) async-start(), calls=%async_computation.4 | async-start | bytes 2359296 | tf_op jit(solution)/shard_map/psum | solution.py:75
  11.2 145.0 %copy-start.4 = (s32[8,3]{0,1:T(4,128)}, s32[8,3]{0,1:T(4,128)S(1)}, u32[]{:S(2)}) copy-start(s32[8,3]{0,1:T(4,128)S(1)} %reduce-window.20) | copy-start | bytes 292
  160.8 4.1 slice-start
  242.6 3.6 copy-start.1
  242.6 3.6 copy-start.2
  249.0 93.7 %copy-start.5 = (bf16[1,2304,720]{1,2,0:T(8,128)(2,1)S(1)}, bf16[1,2304,720]{1,2,0:T(8,128)(2,1)}, u32[]{:S(2)}) copy-start(bf16[1,2304,720]{1,2,0:T(8,128)(2,1)} %param.27) | copy-start | bytes 9953284
  340.9 1.8 copy-start.3
  362.9 8.6 %copy-start.6 = (bf16[2304,8]{0,1:T(8,128)(2,1)S(1)}, bf16[2304,8]{0,1:T(8,128)(2,1)}, u32[]{:S(2)}) copy-start(bf16[2304,8]{0,1:T(8,128)(2,1)} %param.25) | copy-start | bytes 110596
  362.9 78.7 %all-to-all-start.1 = ((bf16[32,20,2304]{2,1,0:T(8,128)(2,1)}), bf16[32,20,2304]{2,1,0:T(8,128)(2,1)}, u32[]{:S(2)}, u32[]{:S(2)}) async-start(bf16[32,20,2304]{2,1,0:T(8,128)(2,1)} %copy.33), calls=%async_computation.1 | async-start | bytes 7077888 | tf_op jit(solution)/shard_map/all_to_all | solution.py:115
  371.2 122.9 %reduce-scatter.4.cloned.1.call-start = ((), (), s32[]{:S(2)}) async-start(), calls=%async_computation.5 | async-start | bytes 1327104
Sparse Core Ops, SparseCore 0:
  10.8 132.5 all-gather.1
  164.9 77.7 all-reduce.1
  448.4 45.6 reduce-scatter.3
where the time goes:
time: 506 us; the launch traced here: 505 us
  blocking collectives  228 us (45%)
  waiting for transfers between devices  192 us (38%)
  matrix products  32.6 us (6%)
  local copies, waits for them, and re-layouts  20.3 us (4%)
  between operations  13.2 us (3%)
  other arithmetic  10.6 us (2%)
  starting transfers between devices  8.62 us (2%)
    all_gather x1, blocking collectives, on_device(): lax.all_gather(adapter_down_maps, 'req', axis=0, tiled=True)  136 us
    all_to_all x1, blocking collectives, on_device(): lax.all_to_all(send_rows, 'req', split_axis=0, concat_axis=0, tiled=True)  91.9 us
    psum x1, waiting for transfers between devices, on_device(): lax.psum(head_part.astype(jnp.bfloat16), 'tp').astype(jnp.float32)  77.7 us
    all_to_all x1, waiting for transfers between devices, on_device(): lax.all_to_all(partial_value.astype(jnp.bfloat16), 'req', split_axis=0, c...  67.8 us
    unnamed x4, waiting for transfers between devices  46.5 us
    dot_general x1, matrix products, on_device(): jnp.einsum('nqf,fd->nqd', hidden, down_local, preferred_element_type=jnp....  11.1 us
  transfers between devices with their start and end apart: 4, of which 3 were waited for; matrix products, arithmetic and copies ran while one was open for 3% of the time, Pallas kernels for 0%

commit v1 on v0

--- a/solution.py
+++ b/solution.py
@@ -1,10 +1,21 @@
+import functools
 import jax
 import jax.numpy as jnp
 from jax import lax
 from jax.sharding import PartitionSpec as P
+from jax.lax import all_to_all, axis_size
 
 CAP = 80
 NORM_EPS = 1e-05
+
+
+def bind_the_tiles(x_in, device_axis):
+    left_arr = jnp.stack([x_in for _ in range(axis_size(device_axis))], axis=0)
+    work_now = all_to_all(left_arr, device_axis, 0, 0)
+    return jnp.concatenate(work_now, axis=0)
+
+
+_fill_loops = functools.partial(bind_the_tiles, device_axis="req")
 
 
 def adapter_onehot(request_token_length, request_adapter_entry, active_count, token_count):
@@ -51,7 +62,7 @@
     adapter_rank_size = adapter_down_maps.shape[2]
     stored_rows = adapter_storage_row[active_adapters]
     all_down, all_up = (
-        lax.all_gather(adapter_down_maps, "req", axis=0, tiled=True),
+        _fill_loops(adapter_down_maps),
         lax.all_gather(adapter_up_maps, "req", axis=0, tiled=True),
     )
     active_down = all_down[stored_rows]

time: 506 us -> 474 us (0.937)
  blocking collectives: 228 us -> 91.9 us
  waiting for transfers between devices: 192 us -> 285 us
  starting transfers between devices: 8.62 us -> 22.9 us
    all_gather x1 -> x0, blocking collectives: 136 us -> none  [on_device(): lax.all_gather(adapter_down_maps, 'req', axis=0, tiled=True)]
    all_gather x1, waiting for transfers between devices: 0.01 us -> 89.3 us  [on_device(): lax.all_gather(adapter_up_maps, 'req', axis=0, tiled=True)]
    all_to_all x0 -> x1, waiting for transfers between devices: none -> 14.5 us  [bind_the_tiles(): work_now = all_to_all(left_arr, device_axis, 0, 0)]
    all_to_all x0 -> x1, starting transfers between devices: none -> 14.3 us  [bind_the_tiles(): work_now = all_to_all(left_arr, device_axis, 0, 0)]
    psum x1, waiting for transfers between devices: 77.7 us -> 69.9 us  [on_device(): lax.psum(head_part.astype(jnp.bfloat16), 'tp').astype(jnp.float32)]
  transfers between devices with their start and end apart: 4 -> 5, of which waited for: 3 -> 5; matrix products, arithmetic and copies ran while one was open for 3% -> 2% of each run, Pallas kernels for 0% -> 0%
where the time goes in v1:
time: 474 us; the launch traced here: 473 us
  waiting for transfers between devices  285 us (60%)
  blocking collectives  91.9 us (19%)
  matrix products  32.5 us (7%)
  starting transfers between devices  22.9 us (5%)
  local copies, waits for them, and re-layouts  20.8 us (4%)
  between operations  13.4 us (3%)
  other arithmetic  6.58 us (1%)
    all_to_all x1, blocking collectives, on_device(): lax.all_to_all(send_rows, 'req', split_axis=0, concat_axis=0, tiled=True)  91.9 us
    all_gather x1, waiting for transfers between devices, on_device(): lax.all_gather(adapter_up_maps, 'req', axis=0, tiled=True)  89.3 us
    psum x1, waiting for transfers between devices, on_device(): lax.psum(head_part.astype(jnp.bfloat16), 'tp').astype(jnp.float32)  69.9 us
    all_to_all x1, waiting for transfers between devices, on_device(): lax.all_to_all(partial_value.astype(jnp.bfloat16), 'req', split_axis=0, c...  65.8 us
    unnamed x4, waiting for transfers between devices  45.6 us
    all_to_all x1, waiting for transfers between devices, bind_the_tiles(): work_now = all_to_all(left_arr, device_axis, 0, 0)  14.5 us
    all_to_all x1, starting transfers between devices, bind_the_tiles(): work_now = all_to_all(left_arr, device_axis, 0, 0)  14.3 us
    dot_general x1, matrix products, on_device(): jnp.einsum('nqf,fd->nqd', hidden, down_local, preferred_element_type=jnp....  11.1 us
  transfers between devices with their start and end apart: 5, of which 5 were waited for; matrix products, arithmetic and copies ran while one was open for 2% of the time, Pallas kernels for 0%

profile of v1, /device:TPU:4, one launch (start us, length us, event | category | flops | bytes accessed | tf_op | source)
XLA Modules:
  0.0 473.2 jit_solution(10943472928631821262)
XLA Ops:
  6.5 0.0 copy-start
  6.5 0.0 copy-start.8
  6.5 0.0 copy-start.13
  6.5 0.0 copy-start.6
  6.5 0.0 copy-start.1
  6.6 0.0 copy-start.9
  6.6 0.0 copy-start.5
  6.6 0.0 all-gather.2.cloned.1.call-start
  6.6 0.7 all-gather.2.cloned.1.call-update
  7.3 1.8 stack.2
  9.2 14.3 %all-to-all-start = ((bf16[32,2,288,16]{2,3,1,0:T(8,128)(2,1)}), bf16[32,2,288,16]{2,3,1,0:T(8,128)(2,1)}, u32[]{:S(2)}, u32[]{:S(2)}) async-start(bf16[32,2,288,16]{2,3,1,0:T(8,128)(2,1)} %stack.2), calls=%async_computation | async-start | bytes 1572864 | tf_op jit(solution)/shard_map/all_to_all | solution.py:14
  23.4 0.0 all-reduce.2.cloned.1.call-start
  23.5 0.0 copy-done.8
  23.5 0.6 reduce-window.19
  24.1 0.2 slice_reduce_fusion
  24.3 0.0 copy-done.12
  24.3 0.0 copy-done.13
  24.4 0.2 reduce-window.18
  24.5 0.0 copy-done.6
  24.6 0.0 copy-start.7
  24.6 0.0 copy-done.1
  24.6 0.7 gather_fusion
  25.3 0.1 convert_reduce_fusion
  25.3 0.0 copy-done.9
  25.4 0.1 select_reduce_fusion.2
  25.4 0.0 copy-done.5
  25.5 3.6 fusion.42
  29.0 14.5 %all-to-all-done = bf16[32,2,288,16]{2,3,1,0:T(8,128)(2,1)} async-done(((bf16[32,2,288,16]{2,3,1,0:T(8,128)(2,1)}), bf16[32,2,288,16]{2,3,1,0:T(8,128)(2,1)}, u32[]{:S(2)}, u32[]{:S(2)}) %all-to-all-start) | async-done | bytes 589856 | tf_op jit(solution)/shard_map/all_to_all | solution.py:14
  43.5 1.7 gather_fusion.1
  45.3 0.0 copy-done.7
  45.3 89.3 %all-gather.2.cloned.1.call-done = bf16[64,16,2304]{2,1,0:T(8,128)(2,1)} async-done(((bf16[2,16,2304]{2,1,0:T(8,128)(2,1)}), bf16[64,16,2304]{2,1,0:T(8,128)(2,1)}) %all-gather.2.cloned.1.call-update) | async-done | bytes 4718608 | tf_op jit(solution)/shard_map/all_gather | solution.py:66
  134.6 4.0 gather_fusion.2
  138.6 0.6 broadcast_in_dim.27
  139.2 0.0 slice-start
  139.2 3.9 fusion.1
  143.2 0.0 all-reduce.2.cloned.1.call-update
  143.2 0.1 copy.34
  143.3 0.0 slice-done
  143.3 0.1 add_bitcast_fusion
  143.4 69.9 %all-reduce.2.cloned.1.call-done = bf16[256,2304]{1,0:T(8,128)(2,1)} async-done(((bf16[256,2304]{1,0:T(8,128)(2,1)}), bf16[256,2304]{1,0:T(8,128)(2,1)}) %all-reduce.2.cloned.1.call-update) | async-done | bytes 1179664 | tf_op jit(solution)/shard_map/psum | solution.py:86
  213.4 3.6 convert_add_fusion
  216.9 0.0 copy-done.2
  216.9 0.0 copy-done.3
  216.9 1.2 convolution_convert_fusion.1
  218.1 1.6 copy.35
  219.7 0.0 copy-start.10
  219.7 91.9 %all_to_all.15 = bf16[32,20,2304]{2,1,0:T(8,128)(2,1)S(1)} all-to-all(bf16[32,20,2304]{2,1,0:T(8,128)(2,1)S(1)} %copy.35), channel_id=1, replica_groups=mesh['req'=32,'tp'=8] {'req'}, dimensions={0} | all-to-all | bytes 5898240 | tf_op jit(solution)/shard_map/all_to_all | solution.py:114
  311.6 1.8 copy-done.4
  313.5 0.0 copy-done.10
  313.5 3.8 fusion.6
  317.2 0.0 copy-done
  317.2 11.1 %convolution_convert_fusion = bf16[32,20,2304]{2,0,1:T(8,128)(2,1)} fusion(bf16[1,720,2304]{2,1,0:T(8,128)(2,1)S(1)} %copy-done, f32[32,20,720]{2,0,1:T(8,128)} %fusion.6, bf16[1,2304,720]{1,2,0:T(8,128)(2,1)} %param.28, bf16[32,20,2304]{2,1,0:T(8,128)(2,1)} %copy-done.4), kind=kOutput, calls=%fused_computation.3 | convolution fusion | flops 4250972160 | bytes 14376960 | tf_op jit(solution)/shard_map/nqf,fd->nqd/dot_general | solution.py:118
  328.3 5.3 %copy.38 = bf16[32,20,2304]{2,1,0:T(8,128)(2,1)} copy(bf16[32,20,2304]{2,0,1:T(8,128)(2,1)} %convolution_convert_fusion) | data formatting | bytes 5898240 | tf_op jit(solution)/shard_map/convert_element_type | solution.py:127
  333.6 8.3 %all-to-all-start.2 = ((bf16[32,20,2304]{2,1,0:T(8,128)(2,1)}), bf16[32,20,2304]{2,1,0:T(8,128)(2,1)}, u32[]{:S(2)}, u32[]{:S(2)}) async-start(bf16[32,20,2304]{2,1,0:T(8,128)(2,1)} %copy.38), calls=%async_computation.2 | async-start | bytes 7077888 | tf_op jit(solution)/shard_map/all_to_all | solution.py:126
  341.9 0.3 reduce-scatter.4.cloned.1.call-start
  342.2 0.0 copy-done.11
  342.2 2.2 select_reduce_fusion.1
  344.5 65.8 %all-to-all-done.2 = bf16[32,20,2304]{2,1,0:T(8,128)(2,1)} async-done(((bf16[32,20,2304]{2,1,0:T(8,128)(2,1)}), bf16[32,20,2304]{2,1,0:T(8,128)(2,1)}, u32[]{:S(2)}, u32[]{:S(2)}) %all-to-all-start.2) | async-done | bytes 2949152 | tf_op jit(solution)/shard_map/all_to_all | solution.py:126
  410.3 6.8 %fusion.2 = bf16[2304,256]{1,0:T(8,128)(2,1)} fusion(bf16[32,20,2304]{2,1,0:T(8,128)(2,1)} %all-to-all-done.2, f32[32,256]{1,0:T(8,128)S(1)} %broadcast_bitcast_fusion, s32[32,20]{0,1:T(8,128)S(1)} %copy.34, s32[32,256]{1,0:T(8,128)S(1)} %broadcast_bitcast_fusion.1, pred[32,256]{1,0:T(8,128)(4,1)S(1)} %broadcast_bitcast_fusion.2), kind=kOutput, calls=%fused_computation.9 | convolution fusion | flops 4530929664 | bytes 4205056 | tf_op jit(solution)/shard_map/hqt,hqd->td/dot_general | solution.py:129
  417.1 0.0 reduce-scatter.4.cloned.1.call-update
  417.1 44.9 %reduce-scatter.4.cloned.1.call-done = bf16[288,256]{1,0:T(8,128)(2,1)} async-done(((bf16[2304,256]{1,0:T(8,128)(2,1)}), bf16[288,256]{1,0:T(8,128)(2,1)}) %reduce-scatter.4.cloned.1.call-update) | async-done | bytes 147472
  462.0 1.1 copy.43
  463.0 1.9 add_convert_fusion
  464.9 1.7 copy.41
  (23 shorter events, 0.1 us)
Async XLA Ops:
  6.5 310.7 %copy-start = (bf16[1,720,2304]{2,1,0:T(8,128)(2,1)S(1)}, bf16[1,720,2304]{2,1,0:T(8,128)(2,1)}, u32[]{:S(2)}) copy-start(bf16[1,720,2304]{2,1,0:T(8,128)(2,1)} %param.29) | copy-start | bytes 9953284
  6.5 16.9 %copy-start.8 = (s32[256,2]{0,1:T(2,128)S(1)}, s32[256,2]{0,1:T(2,128)}, u32[]{:S(2)}) copy-start(s32[256,2]{0,1:T(2,128)} %param.26) | copy-start | bytes 6148
  6.5 17.8 %copy-start.12 = (s32[16]{0:T(128)S(1)}, s32[16]{0:T(128)}, u32[]{:S(2)}) copy-start(s32[16]{0:T(128)} %param.21) | copy-start | bytes 196
  6.5 17.8 %copy-start.13 = (s32[1,4]{1,0:T(1,128)S(1)}, s32[1,4]{1,0:T(1,128)}, u32[]{:S(2)}) copy-start(s32[1,4]{1,0:T(1,128)} %param.22) | copy-start | bytes 52
  6.5 18.0 %copy-start.6 = (bf16[2304]{0:T(1024)(128)(2,1)S(1)}, bf16[2304]{0:T(1024)(128)(2,1)}, u32[]{:S(2)}) copy-start(bf16[2304]{0:T(1024)(128)(2,1)} %param.24) | copy-start | bytes 13828
  6.5 18.0 %copy-start.1 = (s32[64]{0:T(128)S(1)}, s32[64]{0:T(128)}, u32[]{:S(2)}) copy-start(s32[64]{0:T(128)} %param.20) | copy-start | bytes 772
  6.6 18.8 %copy-start.9 = (s32[1,4]{1,0:T(1,128)S(1)}, s32[1,4]{1,0:T(1,128)}, u32[]{:S(2)}) copy-start(s32[1,4]{1,0:T(1,128)} %param.23) | copy-start | bytes 52
  6.6 18.9 %copy-start.5 = (bf16[256,288]{0,1:T(8,128)(2,1)S(1)}, bf16[256,288]{0,1:T(8,128)(2,1)}, u32[]{:S(2)}) copy-start(bf16[256,288]{0,1:T(8,128)(2,1)} %param.16) | copy-start | bytes 442372
  6.6 128.0 %all-gather.2.cloned.1.call-start = ((), (), s32[]{:S(2)}) async-start(), calls=%async_computation.4 | async-start | bytes 4866048 | tf_op jit(solution)/shard_map/all_gather | solution.py:66
  9.2 34.4 %all-to-all-start = ((bf16[32,2,288,16]{2,3,1,0:T(8,128)(2,1)}), bf16[32,2,288,16]{2,3,1,0:T(8,128)(2,1)}, u32[]{:S(2)}, u32[]{:S(2)}) async-start(bf16[32,2,288,16]{2,3,1,0:T(8,128)(2,1)} %stack.2), calls=%async_computation | async-start | bytes 1572864 | tf_op jit(solution)/shard_map/all_to_all | solution.py:14
  23.4 189.9 %all-reduce.2.cloned.1.call-start = ((), (), s32[]{:S(2)}) async-start(), calls=%async_computation.5 | async-start | bytes 2359296 | tf_op jit(solution)/shard_map/psum | solution.py:86
  24.6 20.7 %copy-start.7 = (s32[8,3]{0,1:T(4,128)}, s32[8,3]{0,1:T(4,128)S(1)}, u32[]{:S(2)}) copy-start(s32[8,3]{0,1:T(4,128)S(1)} %reduce-window.20) | copy-start | bytes 292
  139.2 4.1 slice-start
  213.3 3.6 copy-start.2
  213.3 3.6 copy-start.3
  219.7 93.7 %copy-start.10 = (bf16[1,2304,720]{1,2,0:T(8,128)(2,1)S(1)}, bf16[1,2304,720]{1,2,0:T(8,128)(2,1)}, u32[]{:S(2)}) copy-start(bf16[1,2304,720]{1,2,0:T(8,128)(2,1)} %param.27) | copy-start | bytes 9953284
  311.6 1.8 copy-start.4
  333.6 8.6 %copy-start.11 = (bf16[2304,8]{0,1:T(8,128)(2,1)S(1)}, bf16[2304,8]{0,1:T(8,128)(2,1)}, u32[]{:S(2)}) copy-start(bf16[2304,8]{0,1:T(8,128)(2,1)} %param.25) | copy-start | bytes 110596
  333.6 76.6 %all-to-all-start.2 = ((bf16[32,20,2304]{2,1,0:T(8,128)(2,1)}), bf16[32,20,2304]{2,1,0:T(8,128)(2,1)}, u32[]{:S(2)}, u32[]{:S(2)}) async-start(bf16[32,20,2304]{2,1,0:T(8,128)(2,1)} %copy.38), calls=%async_computation.2 | async-start | bytes 7077888 | tf_op jit(solution)/shard_map/all_to_all | solution.py:126
  341.9 120.0 %reduce-scatter.4.cloned.1.call-start = ((), (), s32[]{:S(2)}) async-start(), calls=%async_computation.6 | async-start | bytes 1327104
Sparse Core Ops, SparseCore 0:
  10.9 123.6 all-gather.1
  143.3 69.9 all-reduce.1
  417.2 44.7 reduce-scatter.3
